TPU v7x, 32 devices: a whole 2x2x4 slice. The times are simulated.
32 devices in a mesh: parts: 2 (over x), row: 16 (over z, y, core).
Axes of the slice: x: 2, y: 2, z: 4, core: 2. Of those that a mesh axis runs over, the one named last changes fastest.
Arguments:
- records: bfloat16 [128, 3, 1, 6144], P(('parts', 'row')), parts along dimension 0, may hold values from -120 to 120
- counts: int32 [32], P(('parts', 'row')), parts along dimension 0, may hold values from 1 to 4, 32 in all
- assign: int32 [64], P('parts'), parts along dimension 0, may hold values from 0 to 31, each once
- station_slot: int32 [64], P('parts'), parts along dimension 0, may hold values from 0 to 31, each once
- gap_mask: int32 [64, 1], P('parts'), parts along dimension 0, may hold values 0 or 1
Outputs:
- correlations: float32 [64, 32, 9, 512], P(('parts', 'row')), parts along dimension 0
There are 2 independent parts, one for each index of `parts`. A program takes and returns all parts, laid end to end along the dimension named above; each array names one. Nothing has to cross between parts.
Inputs may be any that keep to these rules, and one draw needn't show every extreme that they name: The counts of one region sum to 32; the largest is 4. `assign`: each station once. `station_slot`: each row once.
All inputs are finite; a program needn't handle non-finite values. No bound on the sum of `counts` on one device may be relied on, other than what follows from the above.
Results may differ from a plain program's by a relative error of at most 0.0073.
Values may be sent and summed in bfloat16 or wider, within the bound.
No kernel may reach another device: no remote copies, remote signals or barrier semaphores. Data moves between devices by JAX's collectives and lax.ppermute only.
A program may use at most 64 MiB of HBM per device.

v0:
```python
import math

import jax
import jax.numpy as jnp
from jax import lax
from jax.sharding import PartitionSpec as P

NFFT = 8192
F = 2048
BAND = 64
LAGS = 512


epsilon_level = 1e-06


def prefix(part, axis, combine, identity):
    place = lax.axis_index(axis)
    gathered = lax.all_gather(part, axis)
    state = jnp.zeros_like(part) + jnp.asarray(identity, part.dtype)

    def one(step, state):
        return combine(state, lax.dynamic_index_in_dim(gathered, step, 0, False))

    return lax.fori_loop(0, place, one, state)


def add_counts(earlier, later):
    return earlier + later


def dft_direct(first_bin, width_bins, samples, length):
    sample = jnp.arange(samples, dtype=jnp.int32)[:, None]
    bin_index = first_bin + jnp.arange(width_bins, dtype=jnp.int32)[None, :]
    phase_index = sample * bin_index % length
    angles = phase_index.astype(jnp.float32) * (2.0 * math.pi / length)
    return jnp.concatenate([jnp.cos(angles), -jnp.sin(angles)], axis=1).astype(jnp.bfloat16)


def lag_table(width_bins, lag_count, length):
    frequency = jnp.arange(width_bins, dtype=jnp.int32)[:, None]
    delays = (jnp.arange(lag_count, dtype=jnp.int32) - lag_count // 2) % length
    phase_index = frequency * delays[None, :] % length
    angles = phase_index.astype(jnp.float32) * (2.0 * math.pi / length)
    return jnp.concatenate([jnp.cos(angles), -jnp.sin(angles)], axis=0).astype(jnp.bfloat16)


def whiten(real_part, imag_part, band_width):
    amplitude = jnp.sqrt(real_part * real_part + imag_part * imag_part)
    full_shape = amplitude.shape
    banded = full_shape[:-1] + (full_shape[-1] // band_width, band_width)
    levels = jnp.mean(amplitude.reshape(banded), axis=-1, keepdims=True)
    levels = jnp.broadcast_to(levels, banded).reshape(full_shape)
    return (real_part / (levels + epsilon_level), imag_part / (levels + epsilon_level))


def cross_pairs(left_rows, right_rows):
    left_real = left_rows[:, None, :, None, :, 0, :].astype(jnp.float32)
    left_imag = left_rows[:, None, :, None, :, 1, :].astype(jnp.float32)
    right_real = right_rows[None, :, None, :, :, 0, :].astype(jnp.float32)
    right_imag = right_rows[None, :, None, :, :, 1, :].astype(jnp.float32)
    real_sum = jnp.sum(left_real * right_real + left_imag * right_imag, axis=4)
    imag_sum = jnp.sum(left_imag * right_real - left_real * right_imag, axis=4)
    return jnp.stack([real_sum, imag_sum], axis=4).astype(jnp.bfloat16)


def project(cross_block, lag_rows):
    row_total = cross_block.shape[0]
    flat_cross = cross_block.reshape(-1, lag_rows.shape[0])
    product = jnp.dot(flat_cross, lag_rows, preferred_element_type=jnp.float32)
    return product.reshape(row_total, -1, 9, lag_rows.shape[1])


def reader_spectra(records, present):
    slot_count, channels, windows, samples = records.shape
    flat_rows = records.reshape(slot_count * channels * windows, samples)
    row_scale = jnp.broadcast_to(present[:, None, :], (slot_count, channels, windows))
    row_scale = row_scale.reshape(-1, 1).astype(jnp.float32)
    width_bins = math.gcd(F, 128)

    def bin_block(first_bin):
        dft_rows = dft_direct(first_bin, width_bins, samples, NFFT)
        product = jnp.dot(flat_rows, dft_rows, preferred_element_type=jnp.float32)
        white_real, white_imag = whiten(product[:, :width_bins], product[:, width_bins:], BAND)
        return jnp.stack([white_real * row_scale, white_imag * row_scale], axis=1).astype(
            jnp.bfloat16
        )

    blocks = lax.map(bin_block, jnp.arange(F // width_bins, dtype=jnp.int32) * width_bins)
    joined = jnp.transpose(blocks, (1, 2, 0, 3))
    return joined.reshape(slot_count, channels, windows, 2, F)


def on_device(records, counts, assign, station_slot, gap_mask):
    slot_count = records.shape[0]
    windows = records.shape[2]
    row_devices = lax.axis_size("row")
    stations = assign.shape[0]
    own_rows = stations // row_devices
    offset = prefix(counts[0], "row", add_counts, jnp.int32(0))
    local_slot = jnp.arange(slot_count, dtype=jnp.int32)
    is_live = local_slot < counts[0]
    global_place = jnp.minimum(offset + local_slot, stations - 1)
    held_station = assign[global_place]
    slot_row = jnp.where(is_live, station_slot[held_station], stations)
    present = gap_mask[held_station] * is_live[:, None].astype(jnp.int32)
    spectra = reader_spectra(records, present)
    positions = jnp.arange(stations, dtype=jnp.int32)
    row_station = jnp.zeros((stations,), jnp.int32).at[station_slot].set(positions)
    present_float = gap_mask[row_station].astype(jnp.float32)
    first_row = lax.axis_index("row") * own_rows
    left_present = lax.dynamic_slice_in_dim(present_float, first_row, own_rows, 0)
    lag_rows = lag_table(F, LAGS, NFFT)
    all_spectra, all_rows = (
        lax.all_gather(spectra, "row", axis=0, tiled=True),
        lax.all_gather(slot_row, "row", axis=0, tiled=True),
    )
    empty_rows = jnp.zeros((stations, 3, windows, 2, F), jnp.bfloat16)
    filled = empty_rows.at[all_rows].set(all_spectra, mode="drop")
    own_block = lax.dynamic_slice_in_dim(filled, first_row, own_rows, 0)
    group_size = math.gcd(stations, 8)
    grouped = filled.reshape(stations // group_size, group_size, 3, windows, 2, F)

    def column_block(right_rows):
        return project(cross_pairs(own_block, right_rows), lag_rows)

    column_lags = lax.map(column_block, grouped)
    raw_lags = jnp.moveaxis(column_lags, 0, 1).reshape(own_rows, stations, 9, LAGS)
    common = jnp.dot(left_present, present_float.T, precision=lax.Precision.HIGHEST)
    return raw_lags / (jnp.maximum(common, 1.0)[:, :, None, None] * math.sqrt(F))


def solution(mesh):
    return jax.shard_map(
        on_device,
        mesh=mesh,
        in_specs=(
            P(("parts", "row"), None, None, None),
            P(("parts", "row")),
            P("parts"),
            P("parts"),
            P("parts", None),
        ),
        out_specs=P(("parts", "row"), None, None, None),
        check_vma=False,
    )
```

profile of v0, /device:TPU:0, one launch (start us, length us, event | category | flops | bytes accessed | tf_op | source)
XLA Modules:
  0.0 386.5 jit_solution(15809229898549284067)
XLA Ops:
  9.2 13.8 %all-reduce = s32[16]{0:T(128)S(1)} all-reduce(s32[16]{0:T(128)S(1)} %dynamic-update-slice), channel_id=1, replica_groups=mesh['parts'=2,'row'=16] {'row'}, use_global_device_ids=true, to_apply=%add | all-reduce | flops 16 | bytes 128
  26.1 242.8 %while.35 = (s32[]{:T(128)}, bf16[16,12,2,128]{3,1,2,0:T(8,128)(2,1)S(1)}, s32[16]{0:T(128)S(1)}, bf16[12,6144]{1,0:T(8,128)(2,1)S(1)}, f32[4]{0:T(128)S(1)}, /*index=5*/s32[]{:T(128)}, f32[]{:T(128)}) while((s32[]{:T(128)}, bf16[16,12,2,128]{3,1,2,0:T(8,128)(2,1)S(1)}, s32[16]{0:T(128)S(1)}, bf16[12,6144]{1,0:T(8,128)(2,1)S(1)}, ...), condition=%wide.region_4.5_spmd.clone, body=%wide.region_2.4_spmd.clone.sunk | while | flops 57437336 | bytes 6549173 | solution.py:89
  27.4 12.8 %cosine_convert_fusion.3 = (bf16[6144,128]{1,0:T(8,128)(2,1)S(1)}, bf16[6144,128]{1,0:T(8,128)(2,1)S(1)}) fusion(s32[128]{0:T(128)S(1)} %iota_add_fusion.2), kind=kLoop, calls=%fused_computation.33.clone.1 | loop fusion | flops 13369344 | bytes 3146240 | tf_op jit(solution)/shard_map/convert.10
  42.5 12.8 %cosine_convert_fusion.3 = (bf16[6144,128]{1,0:T(8,128)(2,1)S(1)}, bf16[6144,128]{1,0:T(8,128)(2,1)S(1)}) fusion(s32[128]{0:T(128)S(1)} %iota_add_fusion.2), kind=kLoop, calls=%fused_computation.33.clone.1 | loop fusion | flops 13369344 | bytes 3146240 | tf_op jit(solution)/shard_map/convert.10
  57.7 12.8 %cosine_convert_fusion.3 = (bf16[6144,128]{1,0:T(8,128)(2,1)S(1)}, bf16[6144,128]{1,0:T(8,128)(2,1)S(1)}) fusion(s32[128]{0:T(128)S(1)} %iota_add_fusion.2), kind=kLoop, calls=%fused_computation.33.clone.1 | loop fusion | flops 13369344 | bytes 3146240 | tf_op jit(solution)/shard_map/convert.10
  72.9 12.8 %cosine_convert_fusion.3 = (bf16[6144,128]{1,0:T(8,128)(2,1)S(1)}, bf16[6144,128]{1,0:T(8,128)(2,1)S(1)}) fusion(s32[128]{0:T(128)S(1)} %iota_add_fusion.2), kind=kLoop, calls=%fused_computation.33.clone.1 | loop fusion | flops 13369344 | bytes 3146240 | tf_op jit(solution)/shard_map/convert.10
  88.1 12.8 %cosine_convert_fusion.3 = (bf16[6144,128]{1,0:T(8,128)(2,1)S(1)}, bf16[6144,128]{1,0:T(8,128)(2,1)S(1)}) fusion(s32[128]{0:T(128)S(1)} %iota_add_fusion.2), kind=kLoop, calls=%fused_computation.33.clone.1 | loop fusion | flops 13369344 | bytes 3146240 | tf_op jit(solution)/shard_map/convert.10
  103.3 12.8 %cosine_convert_fusion.3 = (bf16[6144,128]{1,0:T(8,128)(2,1)S(1)}, bf16[6144,128]{1,0:T(8,128)(2,1)S(1)}) fusion(s32[128]{0:T(128)S(1)} %iota_add_fusion.2), kind=kLoop, calls=%fused_computation.33.clone.1 | loop fusion | flops 13369344 | bytes 3146240 | tf_op jit(solution)/shard_map/convert.10
  118.4 12.8 %cosine_convert_fusion.3 = (bf16[6144,128]{1,0:T(8,128)(2,1)S(1)}, bf16[6144,128]{1,0:T(8,128)(2,1)S(1)}) fusion(s32[128]{0:T(128)S(1)} %iota_add_fusion.2), kind=kLoop, calls=%fused_computation.33.clone.1 | loop fusion | flops 13369344 | bytes 3146240 | tf_op jit(solution)/shard_map/convert.10
  133.6 12.8 %cosine_convert_fusion.3 = (bf16[6144,128]{1,0:T(8,128)(2,1)S(1)}, bf16[6144,128]{1,0:T(8,128)(2,1)S(1)}) fusion(s32[128]{0:T(128)S(1)} %iota_add_fusion.2), kind=kLoop, calls=%fused_computation.33.clone.1 | loop fusion | flops 13369344 | bytes 3146240 | tf_op jit(solution)/shard_map/convert.10
  148.8 12.8 %cosine_convert_fusion.3 = (bf16[6144,128]{1,0:T(8,128)(2,1)S(1)}, bf16[6144,128]{1,0:T(8,128)(2,1)S(1)}) fusion(s32[128]{0:T(128)S(1)} %iota_add_fusion.2), kind=kLoop, calls=%fused_computation.33.clone.1 | loop fusion | flops 13369344 | bytes 3146240 | tf_op jit(solution)/shard_map/convert.10
  164.0 12.8 %cosine_convert_fusion.3 = (bf16[6144,128]{1,0:T(8,128)(2,1)S(1)}, bf16[6144,128]{1,0:T(8,128)(2,1)S(1)}) fusion(s32[128]{0:T(128)S(1)} %iota_add_fusion.2), kind=kLoop, calls=%fused_computation.33.clone.1 | loop fusion | flops 13369344 | bytes 3146240 | tf_op jit(solution)/shard_map/convert.10
  179.1 12.8 %cosine_convert_fusion.3 = (bf16[6144,128]{1,0:T(8,128)(2,1)S(1)}, bf16[6144,128]{1,0:T(8,128)(2,1)S(1)}) fusion(s32[128]{0:T(128)S(1)} %iota_add_fusion.2), kind=kLoop, calls=%fused_computation.33.clone.1 | loop fusion | flops 13369344 | bytes 3146240 | tf_op jit(solution)/shard_map/convert.10
  194.3 12.8 %cosine_convert_fusion.3 = (bf16[6144,128]{1,0:T(8,128)(2,1)S(1)}, bf16[6144,128]{1,0:T(8,128)(2,1)S(1)}) fusion(s32[128]{0:T(128)S(1)} %iota_add_fusion.2), kind=kLoop, calls=%fused_computation.33.clone.1 | loop fusion | flops 13369344 | bytes 3146240 | tf_op jit(solution)/shard_map/convert.10
  209.5 12.8 %cosine_convert_fusion.3 = (bf16[6144,128]{1,0:T(8,128)(2,1)S(1)}, bf16[6144,128]{1,0:T(8,128)(2,1)S(1)}) fusion(s32[128]{0:T(128)S(1)} %iota_add_fusion.2), kind=kLoop, calls=%fused_computation.33.clone.1 | loop fusion | flops 13369344 | bytes 3146240 | tf_op jit(solution)/shard_map/convert.10
  224.7 12.8 %cosine_convert_fusion.3 = (bf16[6144,128]{1,0:T(8,128)(2,1)S(1)}, bf16[6144,128]{1,0:T(8,128)(2,1)S(1)}) fusion(s32[128]{0:T(128)S(1)} %iota_add_fusion.2), kind=kLoop, calls=%fused_computation.33.clone.1 | loop fusion | flops 13369344 | bytes 3146240 | tf_op jit(solution)/shard_map/convert.10
  239.8 12.8 %cosine_convert_fusion.3 = (bf16[6144,128]{1,0:T(8,128)(2,1)S(1)}, bf16[6144,128]{1,0:T(8,128)(2,1)S(1)}) fusion(s32[128]{0:T(128)S(1)} %iota_add_fusion.2), kind=kLoop, calls=%fused_computation.33.clone.1 | loop fusion | flops 13369344 | bytes 3146240 | tf_op jit(solution)/shard_map/convert.10
  255.0 12.8 %cosine_convert_fusion.3 = (bf16[6144,128]{1,0:T(8,128)(2,1)S(1)}, bf16[6144,128]{1,0:T(8,128)(2,1)S(1)}) fusion(s32[128]{0:T(128)S(1)} %iota_add_fusion.2), kind=kLoop, calls=%fused_computation.33.clone.1 | loop fusion | flops 13369344 | bytes 3146240 | tf_op jit(solution)/shard_map/convert.10
  272.6 27.7 %all-reduce.1 = s32[64]{0:T(128)S(1)} all-reduce(s32[64]{0:T(128)S(1)} %fusion.35), channel_id=1, replica_groups=mesh['parts'=2,'row'=16] {'row'}, use_global_device_ids=true, to_apply=%add.1 | all-reduce | flops 64 | bytes 512
  300.3 16.9 %cosine_convert_fusion.1 = (bf16[2048,512]{1,0:T(8,128)(2,1)S(1)}, bf16[2048,512]{1,0:T(8,128)(2,1)S(1)}) fusion(s32[512]{0:T(512)S(1)} %add_select_fusion.2), kind=kLoop, calls=%fused_computation.55 | loop fusion | flops 17825792 | bytes 4196352 | tf_op jit(solution)/shard_map/convert.12
  319.5 6.6 %all-gather.2.cloned.1.call-done = bf16[64,3,1,2,2048]{4,3,2,1,0:T(2,128)(2,1)} async-done(((bf16[4,3,1,2,2048]{4,3,2,1,0:T(2,128)(2,1)}), bf16[64,3,1,2,2048]{4,3,2,1,0:T(2,128)(2,1)}) %all-gather.2.cloned.1.call-update) | async-done | bytes 1572880 | tf_op jit(solution)/shard_map/all_gather | solution.py:115
  326.5 10.1 %scatter_fusion = bf16[32,3,2,2048]{3,2,1,0:T(2,128)(2,1)S(1)} fusion(bf16[32,3,2,2048]{3,2,1,0:T(2,128)(2,1)S(1)} %broadcast.254, s32[64]{0:T(128)S(1)} %compare_select_fusion.2, bf16[64,3,2,2048]{3,2,1,0:T(2,128)(2,1)} %bitcast.97), kind=kCustom, calls=%fused_computation.4 | custom fusion | bytes 4718848 | tf_op jit(solution)/shard_map/scatter | solution.py:119
  336.7 40.4 %while.34 = (s32[]{:T(128)}, f32[4,2,8,9,512]{4,2,3,1,0:T(8,128)}, bf16[2,3,1,2,2048]{4,1,0,3,2:T(4,128)(2,1)S(1)}, bf16[4,8,3,1,2,2048]{5,4,2,1,0,3:T(2,128)(2,1)S(1)}, bf16[4096,512]{1,0:T(8,128)(2,1)}, /*index=5*/s32[]{:T(128)}) while((s32[]{:T(128)}, f32[4,2,8,9,512]{4,2,3,1,0:T(8,128)}, bf16[2,3,1,2,2048]{4,1,0,3,2:T(4,128)(2,1)S(1)}, ...), condition=%wide.region_7.8_spmd, body=%wide.region_6.7_spmd.sunk | while | flops 608821248 | bytes 13582921 | solution.py:127
  373.4 3.7 fusion.55
  (282 shorter events, 87.3 us)
Async XLA Ops:
  6.5 18.9 %copy-start = (s32[32,1]{0,1:T(1,128)S(1)}, s32[32,1]{0,1:T(1,128)}, u32[]{:S(2)}) copy-start(s32[32,1]{0,1:T(1,128)} %param.15) | copy-start | bytes 388
  6.5 319.6 %all-gather.2.cloned.1.call-start = ((), (), s32[]{:S(2)}) async-start(), calls=%async_computation | async-start | bytes 1671168 | tf_op jit(solution)/shard_map/all_gather | solution.py:115
  26.1 243.6 %copy-start.1 = (s32[32]{0:T(128)S(1)}, s32[32]{0:T(128)}, u32[]{:S(2)}) copy-start(s32[32]{0:T(128)} %param.14) | copy-start | bytes 388
Sparse Core Ops, SparseCore 0:
  269.8 56.2 all-gather.1
where the time goes:
time: 387 us; the launch traced here: 386 us
  other arithmetic  261 us (67%)
  blocking collectives  41.4 us (11%)
  local copies, waits for them, and re-layouts  38.5 us (10%)
  matrix products  23.2 us (6%)
  between operations  14.8 us (4%)
  waiting for transfers between devices  6.64 us (2%)
    another operation x21, other arithmetic  231 us
    unnamed x2, blocking collectives  41.4 us
    dot_general x4, matrix products, project(): product = jnp.dot(flat_cross, lag_rows, preferred_element_type=jnp.float32)  14.9 us
    another operation x4, other arithmetic, cross_pairs(): return jnp.stack([real_sum, imag_sum], axis=4).astype(jnp.bfloat16)  10.8 us
    add x16, other arithmetic, dft_direct(): bin_index = first_bin + jnp.arange(width_bins, dtype=jnp.int32)[None, :]  10.3 us
    scatter x1, local copies, waits for them, and re-layouts, on_device(): filled = empty_rows.at[all_rows].set(all_spectra, mode='drop')  10.1 us
    dynamic_slice x16, local copies, waits for them, and re-layouts, reader_spectra(): lax.map(bin_block, jnp.arange(F // width_bins, dtype=jnp.int32) * width_b...  9.38 us
    dot_general x16, matrix products, bin_block(): product = jnp.dot(flat_rows, dft_rows, preferred_element_type=jnp.float32)  8.33 us
  transfers between devices with their start and end apart: 1, of which 1 were waited for; matrix products, arithmetic and copies ran while one was open for 6% of the time, Pallas kernels for 0%

commit v1 on v0

v1 whole, which is shorter than its diff:
```python
import functools
import math

import jax
import jax.numpy as jnp
from jax import lax
from jax.experimental import pallas as pl
from jax.experimental.pallas import tpu as pltpu
from jax.sharding import PartitionSpec as P

NFFT = 8192
F = 2048
BAND = 64
LAGS = 512
EPS = 1e-06

K1 = 64
K2 = F // K1
N2 = NFFT // K1
LANES = 128
META = 16
COLS = 32
F32 = jnp.float32
BF16 = jnp.bfloat16


def iota(shape, dim):
    return lax.broadcasted_iota(jnp.int32, shape, dim)


def cos_sin(phase):
    phase = phase & (NFFT - 1)
    shifted = phase + NFFT // 8
    quadrant = (shifted >> 11) & 3
    angle = ((shifted & 2047) - NFFT // 8).astype(F32) * F32(2.0 * math.pi / NFFT)
    square = angle * angle
    sine = angle * (
        1.0 + square * (-1 / 6 + square * (1 / 120 + square * (-1 / 5040 + square * (1 / 362880))))
    )
    cosine = 1.0 + square * (
        -0.5 + square * (1 / 24 + square * (-1 / 720 + square * (1 / 40320 - square * (1 / 3628800))))
    )
    swap = (quadrant & 1) == 1
    c = jnp.where(swap, sine, cosine)
    s = jnp.where(swap, cosine, sine)
    c = jnp.where((quadrant == 1) | (quadrant == 2), -c, c)
    s = jnp.where(quadrant >= 2, -s, s)
    return c, s


def halves(value):
    high = value.astype(BF16)
    return high, (value - high.astype(F32)).astype(BF16)


def matmul(left, right):
    return jnp.dot(left, right, preferred_element_type=F32)


def matmul_nt(left, right):
    return lax.dot_general(left, right, (((1,), (1,)), ((), ())), preferred_element_type=F32)


def spectra_kernel(slots, counts_ref, x_ref, out_ref):
    channels, depth, _ = x_ref.shape
    k1 = iota((K1, depth), 0)
    column = iota((K1, depth), 1)
    c1, s1 = cos_sin(k1 * (column // slots) * (NFFT // K1))
    owner = column % slots
    rows = [jnp.where(owner == s, t, 0.0) for t in (c1, -s1) for s in range(slots)]
    first = jnp.concatenate(rows, axis=0)
    first = jnp.concatenate(halves(first), axis=1)
    ct, st = cos_sin(iota((K1, N2), 0) * iota((K1, N2), 1))
    ct = jnp.concatenate([ct] * slots, axis=0)
    st = jnp.concatenate([st] * slots, axis=0)
    c2, s2 = cos_sin(iota((K2, N2), 0) * iota((K2, N2), 1) * (NFFT // N2))
    second = jnp.concatenate(
        [jnp.concatenate([c2, s2], axis=1), jnp.concatenate([-s2, c2], axis=1)], axis=0
    )
    second_high, second_low = halves(second)
    second_both = jnp.concatenate([second_high, second_low], axis=0)
    ones = jnp.where(iota((LANES, LANES), 0) // BAND == iota((LANES, LANES), 1) // BAND, 1.0 / BAND, 0.0)
    ones = jnp.concatenate([ones, ones], axis=0).astype(BF16)
    low_lanes = iota((K2, LANES), 1) < K1
    half = slots * K1
    for c in range(channels):
        x = x_ref[c]
        y = matmul(first, jnp.concatenate([x, x], axis=0))
        y_re, y_im = y[:half], y[half:]
        b = jnp.concatenate([y_re * ct + y_im * st, y_im * ct - y_re * st], axis=1)
        b_high, b_low = halves(b)
        z = matmul_nt(second_both, b_high)
        z = z[: 2 * K2] + z[2 * K2 :] + matmul_nt(second_high, b_low)
        for pair in range(slots // 2):
            lanes = slice(pair * LANES, (pair + 1) * LANES)
            re, im = z[:K2, lanes], z[K2:, lanes]
            amplitude = jnp.sqrt(re * re + im * im)
            level = matmul(jnp.concatenate(halves(amplitude), axis=1), ones)
            scale = 1.0 / (level + EPS)
            re, im = re * scale, im * scale
            even = jnp.where(low_lanes, re, pltpu.roll(im, K1, 1))
            odd = jnp.where(low_lanes, pltpu.roll(re, K1, 1), im)
            for s, tile in ((2 * pair, even), (2 * pair + 1, odd)):
                at = (s * channels + c) * K2
                out_ref[at : at + K2, :] = tile.astype(BF16)
    end = slots * channels * K2
    out_ref[end : end + META, :] = jnp.full((META, LANES), counts_ref[0].astype(F32)).astype(BF16)


def lag_kernel(after_ref, out_ref, c2_ref, s2_ref):
    j = iota((K1, LAGS), 1)
    t = (j - LAGS // 2) & (NFFT - 1)
    c1, s1 = cos_sin(iota((K1, LAGS), 0) * t)
    j2 = iota((K2, LAGS), 1)
    t2 = (j2 - LAGS // 2) & (NFFT - 1)
    c2_ref[...], s2_ref[...] = cos_sin(iota((K2, LAGS), 0) * t2 * K1)

    def block(k2, carry):
        c2 = c2_ref[pl.ds(k2, 1), :]
        s2 = s2_ref[pl.ds(k2, 1), :]
        both = jnp.concatenate([c1 * c2 - s1 * s2, -(s1 * c2 + c1 * s2)], axis=0)
        out_ref[pl.ds(pl.multiple_of(k2 * 2 * K1, 2 * K1), 2 * K1), :] = both.astype(BF16)
        return carry

    lax.fori_loop(0, K2, block, 0)


def correlate_kernel(
    masks, slots, channels, own, stations, chunk,
    place_ref, assign_ref, row_ref, gap_ref, lag_ref, *refs
):
    blocks = refs[: len(masks) if masks else 1]
    out_ref, b_ref, a_ref, present_ref, left_ref, acc_ref = refs[len(blocks) :]
    groups = stations // COLS
    stride = channels * COLS
    size = slots * channels * K2 + META
    meta = slots * channels * K2
    lane = iota((8, LANES), 1)
    me = place_ref[0]

    def counted(ref, base, source):
        tile = ref[pl.ds(pl.multiple_of(base + meta, META), META), :].astype(F32)
        return jnp.where(lane == source, tile[:8], 0.0)

    if masks:
        sources = [me ^ mask for mask in masks]
        table = functools.reduce(
            jnp.add, [counted(ref, 0, source) for ref, source in zip(blocks, sources)]
        )
    else:
        total = blocks[0].shape[0] // size
        table = lax.fori_loop(
            0, total, lambda o, v: v + counted(blocks[0], o * size, o), jnp.zeros((8, LANES), F32)
        )

    def spread(ref, base, source):
        offset = (jnp.sum(jnp.where(lane < source, table, 0.0)) / 8.0).astype(jnp.int32)
        count = (jnp.sum(jnp.where(lane == source, table, 0.0)) / 8.0).astype(jnp.int32)
        for s in range(slots):
            @pl.when(s < count)
            def _():
                station = assign_ref[jnp.minimum(offset + s, stations - 1)]
                row = row_ref[station]
                mask = gap_ref[station].astype(F32)
                group, column = row // COLS, row % COLS
                present_ref[pl.ds(row, 1), :] = jnp.full((1, LANES), mask)
                for c in range(channels):
                    at = base + (s * channels + c) * K2
                    tile = ref[pl.ds(pl.multiple_of(at, 16), K2), :].astype(F32) * mask
                    start = group * (K2 * stride) + c * COLS + column
                    b_ref[pl.ds(start, K2, stride=stride), :] = tile

    if masks:
        for ref, source in zip(blocks, sources):
            spread(ref, 0, source)
    else:
        lax.fori_loop(0, total, lambda o, v: (spread(blocks[0], o * size, o), v)[1], 0)

    low = iota((K2, LANES), 1) < K1
    for a in range(own):
        row = me * own + a
        group, column = row // COLS, row % COLS
        for c in range(channels):
            start = group * (K2 * stride) + c * COLS + column
            tile = b_ref[pl.ds(start, K2, stride=stride), :]
            q = a * channels + c
            swapped = pltpu.roll(tile, K1, 1)
            a_ref[q, :K2, :] = jnp.where(low, tile, -swapped)
            a_ref[q, K2:, :] = jnp.where(low, swapped, tile)

    rows = own * channels
    width = chunk * LANES

    def column_group(group, carry):
        for step in range(K2 // chunk):
            for kk in range(chunk):
                k2 = step * chunk + kk
                base = pl.multiple_of(group * (K2 * stride) + k2 * stride, 8)
                b = b_ref[pl.ds(base, stride), :]
                b_swapped = pltpu.roll(b, K1, 1)
                for q in range(rows):
                    cross = a_ref[q, k2 : k2 + 1, :] * b + a_ref[q, K2 + k2 : K2 + k2 + 1, :] * b_swapped
                    left_ref[step % 2, q * stride : (q + 1) * stride, kk * LANES : (kk + 1) * LANES] = (
                        cross.astype(BF16)
                    )
            product = matmul(left_ref[step % 2], lag_ref[step * width : (step + 1) * width, :])
            if step == 0:
                acc_ref[...] = product
            else:
                acc_ref[...] += product
        for a in range(own):
            first = pl.multiple_of(group * COLS, 8)
            common = present_ref[pl.ds(first, COLS), :] * present_ref[pl.ds(me * own + a, 1), :]
            scale = 1.0 / (jnp.maximum(common, 1.0) * math.sqrt(F))
            scale = jnp.concatenate([scale] * (LAGS // LANES), axis=1)
            for c in range(channels):
                for d in range(channels):
                    at = (a * channels + c) * stride + d * COLS
                    out_ref[a, channels * c + d, pl.ds(first, COLS), :] = acc_ref[at : at + COLS, :] * scale
        return carry

    if groups == 1:
        column_group(0, 0)
    else:
        lax.fori_loop(0, groups, column_group, 0)


def swap_with(bits, total):
    return [(i, i ^ bits) for i in range(total)]


def gather_blocks(block, total):
    if total != 16:
        return [lax.all_gather(block, "row", axis=0, tiled=True)], None

    def send(value, bits):
        return lax.ppermute(value, "row", swap_with(bits, total))

    far = send(block, 8)
    near = [(block, 0), (far, 8)]
    for bits in (4, 2, 6):
        near.append((send(block, bits), bits))
    for bits in (4, 2, 6):
        near.append((send(far, bits), 8 ^ bits))
    near += [(send(value, 1), bits ^ 1) for value, bits in near]
    return [value for value, _ in near], tuple(bits for _, bits in near)


def whole_spec(space):
    return pl.BlockSpec(memory_space=space)


def on_device(records, counts, assign, station_slot, gap_mask):
    slots, channels, windows, samples = records.shape
    stations = assign.shape[0]
    total = lax.axis_size("row")
    own = stations // total
    assert windows == 1 and slots % 2 == 0 and samples % LANES == 0 and stations % COLS == 0
    depth = samples // LANES
    x = jnp.transpose(records.reshape(slots, channels, depth, LANES), (1, 2, 0, 3))
    x = x.reshape(channels, depth * slots, LANES)
    size = slots * channels * K2 + META
    block = pl.pallas_call(
        functools.partial(spectra_kernel, slots),
        out_shape=jax.ShapeDtypeStruct((size, LANES), BF16),
        in_specs=[whole_spec(pltpu.SMEM), whole_spec(pltpu.VMEM)],
        out_specs=whole_spec(pltpu.VMEM),
        compiler_params=pltpu.CompilerParams(vmem_limit_bytes=16 << 20),
        cost_estimate=pl.CostEstimate(flops=1 << 29, bytes_accessed=1 << 19, transcendentals=0),
        name="spectra",
    )(counts, x)
    lag_rows = pl.pallas_call(
        lag_kernel,
        out_shape=jax.ShapeDtypeStruct((2 * F, LAGS), BF16),
        in_specs=[whole_spec(pl.ANY)],
        out_specs=whole_spec(pltpu.VMEM),
        scratch_shapes=[pltpu.VMEM((K2, LAGS), F32), pltpu.VMEM((K2, LAGS), F32)],
        compiler_params=pltpu.CompilerParams(vmem_limit_bytes=16 << 20),
        cost_estimate=pl.CostEstimate(flops=1 << 24, bytes_accessed=1 << 22, transcendentals=0),
        name="lag_rows",
    )(block)
    blocks, masks = gather_blocks(block, total)
    place = lax.axis_index("row").astype(jnp.int32).reshape(1)
    chunk = 8
    rows = own * channels
    stride = channels * COLS
    product = pl.pallas_call(
        functools.partial(correlate_kernel, masks, slots, channels, own, stations, chunk),
        out_shape=jax.ShapeDtypeStruct((own, channels * channels, stations, LAGS), F32),
        in_specs=[whole_spec(pltpu.SMEM)] * 4 + [whole_spec(pltpu.VMEM)] * (1 + len(blocks)),
        out_specs=whole_spec(pltpu.VMEM),
        scratch_shapes=[
            pltpu.VMEM((stations // COLS * K2 * stride, LANES), F32),
            pltpu.VMEM((rows, 2 * K2, LANES), F32),
            pltpu.VMEM((stations, LANES), F32),
            pltpu.VMEM((2, rows * stride, chunk * LANES), BF16),
            pltpu.VMEM((rows * stride, LAGS), F32),
        ],
        compiler_params=pltpu.CompilerParams(vmem_limit_bytes=40 << 20),
        cost_estimate=pl.CostEstimate(flops=1 << 31, bytes_accessed=8 << 20, transcendentals=0),
        name="correlate",
    )(place, assign, station_slot, gap_mask.reshape(stations), lag_rows, *blocks)
    return jnp.swapaxes(product, 1, 2)


def solution(mesh):
    return jax.shard_map(
        on_device,
        mesh=mesh,
        in_specs=(
            P(("parts", "row"), None, None, None),
            P(("parts", "row")),
            P("parts"),
            P("parts"),
            P("parts", None),
        ),
        out_specs=P(("parts", "row"), None, None, None),
        check_vma=False,
    )
```

time: 387 us -> 33.5 us (0.09)
  other arithmetic: 261 us -> 0 us
  blocking collectives: 41.4 us -> 0 us
  local copies, waits for them, and re-layouts: 38.5 us -> 0.91 us
  matrix products: 23.2 us -> 0 us
  between operations: 14.8 us -> 0.79 us
  Pallas kernels: 0 us -> 12.5 us
  starting transfers between devices: 0.01 us -> 12.1 us
    another operation x41 -> x0, other arithmetic: 243 us -> none
    unnamed x2 -> x0, blocking collectives: 41.4 us -> none
    dot_general x20 -> x0, matrix products: 23.2 us -> none  [the longest x4 14.9 us: project(): product = jnp.dot(flat_cross, lag_rows, preferred_element_type=jnp.float32)]
    pallas_call x0 -> x3, Pallas kernels: none -> 12.5 us  [the longest x1 9.07 us: on_device(): pl.pallas_call(functools.partial(correlate_kernel, masks, slots, channels...]
    ppermute x0 -> x15, starting transfers between devices: none -> 12.1 us  [send(): return lax.ppermute(value, 'row', swap_with(bits, total))]
    scatter x2 -> x0, local copies, waits for them, and re-layouts: 10.8 us -> none  [the longest x1 10.1 us: on_device(): filled = empty_rows.at[all_rows].set(all_spectra, mode='drop')]
    add x32 -> x0, other arithmetic: 10.4 us -> none  [the longest x16 10.3 us: dft_direct(): bin_index = first_bin + jnp.arange(width_bins, dtype=jnp.int32)[None, :]]
    dynamic_slice x25 -> x0, local copies, waits for them, and re-layouts: 10.2 us -> none  [the longest x16 9.38 us: reader_spectra(): lax.map(bin_block, jnp.arange(F // width_bins, dtype=jnp.int32) * width_b...]
  transfers between devices with their start and end apart: 1 -> 15, of which waited for: 1 -> 5; matrix products, arithmetic and copies ran while one was open for 6% -> 0% of each run, Pallas kernels for 0% -> 5%
where the time goes in v1:
time: 33.5 us; the launch traced here: 33.3 us
  Pallas kernels  12.5 us (37%)
  starting transfers between devices  12.1 us (36%)
  waiting for transfers between devices  7.08 us (21%)
  local copies, waits for them, and re-layouts  0.91 us (3%)
  between operations  0.79 us (2%)
    ppermute x15, starting transfers between devices, send(): return lax.ppermute(value, 'row', swap_with(bits, total))  12.1 us
    pallas_call x1, Pallas kernels, on_device(): pl.pallas_call(functools.partial(correlate_kernel, masks, slots, channels...  9.07 us
    ppermute x15, waiting for transfers between devices, send(): return lax.ppermute(value, 'row', swap_with(bits, total))  7.08 us
    pallas_call x1, Pallas kernels, on_device(): pl.pallas_call(functools.partial(spectra_kernel, slots), out_shape=jax.Sh...  1.88 us
    pallas_call x1, Pallas kernels, on_device(): pl.pallas_call(lag_kernel, out_shape=jax.ShapeDtypeStruct((2 * F, LAGS),...  1.55 us
    unnamed x8, local copies, waits for them, and re-layouts  0.91 us
  transfers between devices with their start and end apart: 15, of which 5 were waited for; matrix products, arithmetic and copies ran while one was open for 0% of the time, Pallas kernels for 5%

profile of v1, /device:TPU:0, one launch (start us, length us, event | category | flops | bytes accessed | tf_op | source)
XLA Modules:
  0.0 33.3 jit_solution(14149705321637884494)
XLA Ops:
  0.7 0.9 %copy-done = bf16[4,3,1,6144]{3,0,2,1:T(4,128)(2,1)S(1)} copy-done((bf16[4,3,1,6144]{3,0,2,1:T(4,128)(2,1)S(1)}, bf16[4,3,1,6144]{3,0,2,1:T(4,128)(2,1)}, u32[]{:S(2)}) %copy-start) | copy-done | bytes 147480
  1.6 1.9 %spectra.1.after_ref.refs_0_ = bf16[400,128]{1,0:T(8,128)(2,1)S(1)} custom-call(s32[1]{0:T(128)S(6)} %copy.7.counts_ref, bf16[3,192,128]{2,1,0:T(8,128)(2,1)S(1)} %bitcast.8), custom_call_target="tpu_custom_call" | custom-call | flops 536870912 | bytes 524288 | tf_op jit(solution)/shard_map/spectra/pallas_call | solution.py:263
  3.5 4.1 %collective-permute-start.3 = (bf16[400,128]{1,0:T(8,128)(2,1)S(1)}, bf16[400,128]{1,0:T(8,128)(2,1)S(1)}, u32[]{:S(2)}, u32[]{:S(2)}) collective-permute-start(bf16[400,128]{1,0:T(8,128)(2,1)S(1)} %spectra.1.after_ref.refs_0_), channel_id=1, source_target_pairs={{0,6},{1,7},{2,4},{3,5},{4,2},{5,3},{6,0},{7,1},{8,14},{9,15},{10,... | collective-permute-start | bytes 307208 | tf_op jit(solution)/shard_map/ppermute | solution.py:237
  7.6 0.5 %collective-permute-start.2 = (bf16[400,128]{1,0:T(8,128)(2,1)S(1)}, bf16[400,128]{1,0:T(8,128)(2,1)S(1)}, u32[]{:S(2)}, u32[]{:S(2)}) collective-permute-start(bf16[400,128]{1,0:T(8,128)(2,1)S(1)} %spectra.1.after_ref.refs_0_), channel_id=1, source_target_pairs={{0,2},{1,3},{2,0},{3,1},{4,6},{5,7},{6,4},{7,5},{8,10},{9,11},{10,... | collective-permute-start | bytes 307208 | tf_op jit(solution)/shard_map/ppermute | solution.py:237
  8.1 2.6 %collective-permute-start = (bf16[400,128]{1,0:T(8,128)(2,1)S(1)}, bf16[400,128]{1,0:T(8,128)(2,1)S(1)}, u32[]{:S(2)}, u32[]{:S(2)}) collective-permute-start(bf16[400,128]{1,0:T(8,128)(2,1)S(1)} %spectra.1.after_ref.refs_0_), channel_id=1, source_target_pairs={{0,8},{1,9},{2,10},{3,11},{4,12},{5,13},{6,14},{7,15},{8,0},{9,1},... | collective-permute-start | bytes 307208 | tf_op jit(solution)/shard_map/ppermute | solution.py:237
  10.7 0.0 collective-permute-start.7
  10.7 0.5 %collective-permute-start.1 = (bf16[400,128]{1,0:T(8,128)(2,1)S(1)}, bf16[400,128]{1,0:T(8,128)(2,1)S(1)}, u32[]{:S(2)}, u32[]{:S(2)}) collective-permute-start(bf16[400,128]{1,0:T(8,128)(2,1)S(1)} %spectra.1.after_ref.refs_0_), channel_id=1, source_target_pairs={{0,4},{1,5},{2,6},{3,7},{4,0},{5,1},{6,2},{7,3},{8,12},{9,13},{10,... | collective-permute-start | bytes 307208 | tf_op jit(solution)/shard_map/ppermute | solution.py:237
  11.1 0.2 collective-permute-start.11
  11.3 1.3 %collective-permute-done.2.refs_3_ = bf16[400,128]{1,0:T(8,128)(2,1)S(1)} collective-permute-done((bf16[400,128]{1,0:T(8,128)(2,1)S(1)}, bf16[400,128]{1,0:T(8,128)(2,1)S(1)}, u32[]{:S(2)}, u32[]{:S(2)}) %collective-permute-start.2) | collective-permute-done | bytes 102432 | tf_op jit(solution)/shard_map/ppermute | solution.py:237
  12.7 0.0 collective-permute-start.10
  12.7 2.0 %collective-permute-done.refs_1_ = bf16[400,128]{1,0:T(8,128)(2,1)S(1)} collective-permute-done((bf16[400,128]{1,0:T(8,128)(2,1)S(1)}, bf16[400,128]{1,0:T(8,128)(2,1)S(1)}, u32[]{:S(2)}, u32[]{:S(2)}) %collective-permute-start) | collective-permute-done | bytes 102432 | tf_op jit(solution)/shard_map/ppermute | solution.py:237
  14.6 1.1 %collective-permute-start.6 = (bf16[400,128]{1,0:T(8,128)(2,1)S(1)}, bf16[400,128]{1,0:T(8,128)(2,1)S(1)}, u32[]{:S(2)}, u32[]{:S(2)}) collective-permute-start(bf16[400,128]{1,0:T(8,128)(2,1)S(1)} %collective-permute-done.refs_1_), channel_id=1, source_target_pairs={{0,6},{1,7},{2,4},{3,5},{4,2},{5,3},{6,0},{7,1},{8,14},{9,15},{10,... | collective-permute-start | bytes 307208 | tf_op jit(solution)/shard_map/ppermute | solution.py:237
  15.7 2.2 %collective-permute-start.5 = (bf16[400,128]{1,0:T(8,128)(2,1)S(1)}, bf16[400,128]{1,0:T(8,128)(2,1)S(1)}, u32[]{:S(2)}, u32[]{:S(2)}) collective-permute-start(bf16[400,128]{1,0:T(8,128)(2,1)S(1)} %collective-permute-done.refs_1_), channel_id=1, source_target_pairs={{0,2},{1,3},{2,0},{3,1},{4,6},{5,7},{6,4},{7,5},{8,10},{9,11},{10,... | collective-permute-start | bytes 307208 | tf_op jit(solution)/shard_map/ppermute | solution.py:237
  18.0 0.0 collective-permute-done.1.refs_2_
  18.0 0.4 %collective-permute-start.4 = (bf16[400,128]{1,0:T(8,128)(2,1)S(1)}, bf16[400,128]{1,0:T(8,128)(2,1)S(1)}, u32[]{:S(2)}, u32[]{:S(2)}) collective-permute-start(bf16[400,128]{1,0:T(8,128)(2,1)S(1)} %collective-permute-done.refs_1_), channel_id=1, source_target_pairs={{0,4},{1,5},{2,6},{3,7},{4,0},{5,1},{6,2},{7,3},{8,12},{9,13},{10,... | collective-permute-start | bytes 307208 | tf_op jit(solution)/shard_map/ppermute | solution.py:237
  18.3 0.0 collective-permute-done.11.refs_12_
  18.3 0.0 collective-permute-start.8
  18.3 0.0 collective-permute-done.10.refs_11_
  18.4 0.5 %collective-permute-start.9 = (bf16[400,128]{1,0:T(8,128)(2,1)S(1)}, bf16[400,128]{1,0:T(8,128)(2,1)S(1)}, u32[]{:S(2)}, u32[]{:S(2)}) collective-permute-start(bf16[400,128]{1,0:T(8,128)(2,1)S(1)} %collective-permute-done.1.refs_2_), channel_id=1, source_target_pairs={{0,1},{1,0},{2,3},{3,2},{4,5},{5,4},{6,7},{7,6},{8,9},{9,8},{10,11... | collective-permute-start | bytes 307208 | tf_op jit(solution)/shard_map/ppermute | solution.py:237
  18.9 1.6 %collective-permute-done.6.refs_7_ = bf16[400,128]{1,0:T(8,128)(2,1)S(1)} collective-permute-done((bf16[400,128]{1,0:T(8,128)(2,1)S(1)}, bf16[400,128]{1,0:T(8,128)(2,1)S(1)}, u32[]{:S(2)}, u32[]{:S(2)}) %collective-permute-start.6) | collective-permute-done | bytes 102432 | tf_op jit(solution)/shard_map/ppermute | solution.py:237
  20.4 1.3 %collective-permute-done.5.refs_6_ = bf16[400,128]{1,0:T(8,128)(2,1)S(1)} collective-permute-done((bf16[400,128]{1,0:T(8,128)(2,1)S(1)}, bf16[400,128]{1,0:T(8,128)(2,1)S(1)}, u32[]{:S(2)}, u32[]{:S(2)}) %collective-permute-start.5) | collective-permute-done | bytes 102432 | tf_op jit(solution)/shard_map/ppermute | solution.py:237
  21.7 0.9 %collective-permute-done.4.refs_5_ = bf16[400,128]{1,0:T(8,128)(2,1)S(1)} collective-permute-done((bf16[400,128]{1,0:T(8,128)(2,1)S(1)}, bf16[400,128]{1,0:T(8,128)(2,1)S(1)}, u32[]{:S(2)}, u32[]{:S(2)}) %collective-permute-start.4) | collective-permute-done | bytes 102432 | tf_op jit(solution)/shard_map/ppermute | solution.py:237
  22.6 1.6 %lag_rows.1.lag_ref = bf16[4096,512]{1,0:T(8,128)(2,1)S(1)} custom-call(bf16[400,128]{1,0:T(8,128)(2,1)S(1)} %spectra.1.after_ref.refs_0_), custom_call_target="tpu_custom_call" | custom-call | flops 16777216 | bytes 4194304 | tf_op jit(solution)/shard_map/lag_rows/pallas_call | solution.py:272
  24.3 9.1 %correlate.1 = f32[2,9,32,512]{3,2,1,0:T(8,128)} custom-call(s32[1]{0:T(128)} %bitcast.place_ref, s32[32]{0:T(128)S(1)} %copy-done.1, s32[32]{0:T(128)S(1)} %copy-done.2, s32[32]{0:T(128)S(1)} %bitcast.9, bf16[4096,512]{1,0:T(8,128)(2,1)S(1)} %lag_rows.1.lag_ref, bf16[400,128]{1,0:T(8,128)(2,1)S(1)} %spectra.1.after_ref.refs_0_, ...), custom_call_target="tpu_custom_call" | custom-call | flops 2147483648 | bytes 8388608 | tf_op jit(solution)/shard_map/correlate/pallas_call | solution.py:287
  (17 shorter events, 0.0 us)
Async XLA Ops:
  0.0 24.2 %copy-start.3 = (s32[32,1]{0,1:T(1,128)S(1)}, s32[32,1]{0,1:T(1,128)}, u32[]{:S(2)}) copy-start(s32[32,1]{0,1:T(1,128)} %param.9) | copy-start | bytes 388
  0.0 24.2 %copy-start.2 = (s32[32]{0:T(128)S(1)}, s32[32]{0:T(128)}, u32[]{:S(2)}) copy-start(s32[32]{0:T(128)} %row_ref.1) | copy-start | bytes 388
  0.0 24.3 %copy-start.1 = (s32[32]{0:T(128)S(1)}, s32[32]{0:T(128)}, u32[]{:S(2)}) copy-start(s32[32]{0:T(128)} %assign_ref.1) | copy-start | bytes 388
  0.7 0.9 %copy-start = (bf16[4,3,1,6144]{3,0,2,1:T(4,128)(2,1)S(1)}, bf16[4,3,1,6144]{3,0,2,1:T(4,128)(2,1)}, u32[]{:S(2)}) copy-start(bf16[4,3,1,6144]{3,0,2,1:T(4,128)(2,1)} %param.5) | copy-start | bytes 442372
  3.5 7.6 %collective-permute-start.3 = (bf16[400,128]{1,0:T(8,128)(2,1)S(1)}, bf16[400,128]{1,0:T(8,128)(2,1)S(1)}, u32[]{:S(2)}, u32[]{:S(2)}) collective-permute-start(bf16[400,128]{1,0:T(8,128)(2,1)S(1)} %spectra.1.after_ref.refs_0_), channel_id=1, source_target_pairs={{0,6},{1,7},{2,4},{3,5},{4,2},{5,3},{6,0},{7,1},{8,14},{9,15},{10,... | collective-permute-start | bytes 307208 | tf_op jit(solution)/shard_map/ppermute | solution.py:237
  7.6 5.1 %collective-permute-start.2 = (bf16[400,128]{1,0:T(8,128)(2,1)S(1)}, bf16[400,128]{1,0:T(8,128)(2,1)S(1)}, u32[]{:S(2)}, u32[]{:S(2)}) collective-permute-start(bf16[400,128]{1,0:T(8,128)(2,1)S(1)} %spectra.1.after_ref.refs_0_), channel_id=1, source_target_pairs={{0,2},{1,3},{2,0},{3,1},{4,6},{5,7},{6,4},{7,5},{8,10},{9,11},{10,... | collective-permute-start | bytes 307208 | tf_op jit(solution)/shard_map/ppermute | solution.py:237
  8.1 6.6 %collective-permute-start = (bf16[400,128]{1,0:T(8,128)(2,1)S(1)}, bf16[400,128]{1,0:T(8,128)(2,1)S(1)}, u32[]{:S(2)}, u32[]{:S(2)}) collective-permute-start(bf16[400,128]{1,0:T(8,128)(2,1)S(1)} %spectra.1.after_ref.refs_0_), channel_id=1, source_target_pairs={{0,8},{1,9},{2,10},{3,11},{4,12},{5,13},{6,14},{7,15},{8,0},{9,1},... | collective-permute-start | bytes 307208 | tf_op jit(solution)/shard_map/ppermute | solution.py:237
  10.7 5.1 %collective-permute-start.7 = (bf16[400,128]{1,0:T(8,128)(2,1)S(1)}, bf16[400,128]{1,0:T(8,128)(2,1)S(1)}, u32[]{:S(2)}, u32[]{:S(2)}) collective-permute-start(bf16[400,128]{1,0:T(8,128)(2,1)S(1)} %spectra.1.after_ref.refs_0_), channel_id=1, source_target_pairs={{0,1},{1,0},{2,3},{3,2},{4,5},{5,4},{6,7},{7,6},{8,9},{9,8},{10,11... | collective-permute-start | bytes 307208 | tf_op jit(solution)/shard_map/ppermute | solution.py:237
  10.7 7.3 %collective-permute-start.1 = (bf16[400,128]{1,0:T(8,128)(2,1)S(1)}, bf16[400,128]{1,0:T(8,128)(2,1)S(1)}, u32[]{:S(2)}, u32[]{:S(2)}) collective-permute-start(bf16[400,128]{1,0:T(8,128)(2,1)S(1)} %spectra.1.after_ref.refs_0_), channel_id=1, source_target_pairs={{0,4},{1,5},{2,6},{3,7},{4,0},{5,1},{6,2},{7,3},{8,12},{9,13},{10,... | collective-permute-start | bytes 307208 | tf_op jit(solution)/shard_map/ppermute | solution.py:237
  11.1 7.2 %collective-permute-start.11 = (bf16[400,128]{1,0:T(8,128)(2,1)S(1)}, bf16[400,128]{1,0:T(8,128)(2,1)S(1)}, u32[]{:S(2)}, u32[]{:S(2)}) collective-permute-start(bf16[400,128]{1,0:T(8,128)(2,1)S(1)} %collective-permute-done.3.refs_4_), channel_id=1, source_target_pairs={{0,1},{1,0},{2,3},{3,2},{4,5},{5,4},{6,7},{7,6},{8,9},{9,8},{10,11... | collective-permute-start | bytes 307208 | tf_op jit(solution)/shard_map/ppermute | solution.py:237
  12.7 5.7 %collective-permute-start.10 = (bf16[400,128]{1,0:T(8,128)(2,1)S(1)}, bf16[400,128]{1,0:T(8,128)(2,1)S(1)}, u32[]{:S(2)}, u32[]{:S(2)}) collective-permute-start(bf16[400,128]{1,0:T(8,128)(2,1)S(1)} %collective-permute-done.2.refs_3_), channel_id=1, source_target_pairs={{0,1},{1,0},{2,3},{3,2},{4,5},{5,4},{6,7},{7,6},{8,9},{9,8},{10,11... | collective-permute-start | bytes 307208 | tf_op jit(solution)/shard_map/ppermute | solution.py:237
  14.6 5.8 %collective-permute-start.6 = (bf16[400,128]{1,0:T(8,128)(2,1)S(1)}, bf16[400,128]{1,0:T(8,128)(2,1)S(1)}, u32[]{:S(2)}, u32[]{:S(2)}) collective-permute-start(bf16[400,128]{1,0:T(8,128)(2,1)S(1)} %collective-permute-done.refs_1_), channel_id=1, source_target_pairs={{0,6},{1,7},{2,4},{3,5},{4,2},{5,3},{6,0},{7,1},{8,14},{9,15},{10,... | collective-permute-start | bytes 307208 | tf_op jit(solution)/shard_map/ppermute | solution.py:237
  15.7 6.0 %collective-permute-start.5 = (bf16[400,128]{1,0:T(8,128)(2,1)S(1)}, bf16[400,128]{1,0:T(8,128)(2,1)S(1)}, u32[]{:S(2)}, u32[]{:S(2)}) collective-permute-start(bf16[400,128]{1,0:T(8,128)(2,1)S(1)} %collective-permute-done.refs_1_), channel_id=1, source_target_pairs={{0,2},{1,3},{2,0},{3,1},{4,6},{5,7},{6,4},{7,5},{8,10},{9,11},{10,... | collective-permute-start | bytes 307208 | tf_op jit(solution)/shard_map/ppermute | solution.py:237
  18.0 4.7 %collective-permute-start.4 = (bf16[400,128]{1,0:T(8,128)(2,1)S(1)}, bf16[400,128]{1,0:T(8,128)(2,1)S(1)}, u32[]{:S(2)}, u32[]{:S(2)}) collective-permute-start(bf16[400,128]{1,0:T(8,128)(2,1)S(1)} %collective-permute-done.refs_1_), channel_id=1, source_target_pairs={{0,4},{1,5},{2,6},{3,7},{4,0},{5,1},{6,2},{7,3},{8,12},{9,13},{10,... | collective-permute-start | bytes 307208 | tf_op jit(solution)/shard_map/ppermute | solution.py:237
  18.3 5.9 %collective-permute-start.8 = (bf16[400,128]{1,0:T(8,128)(2,1)S(1)}, bf16[400,128]{1,0:T(8,128)(2,1)S(1)}, u32[]{:S(2)}, u32[]{:S(2)}) collective-permute-start(bf16[400,128]{1,0:T(8,128)(2,1)S(1)} %collective-permute-done.refs_1_), channel_id=1, source_target_pairs={{0,1},{1,0},{2,3},{3,2},{4,5},{5,4},{6,7},{7,6},{8,9},{9,8},{10,11... | collective-permute-start | bytes 307208 | tf_op jit(solution)/shard_map/ppermute | solution.py:237
  18.4 5.8 %collective-permute-start.9 = (bf16[400,128]{1,0:T(8,128)(2,1)S(1)}, bf16[400,128]{1,0:T(8,128)(2,1)S(1)}, u32[]{:S(2)}, u32[]{:S(2)}) collective-permute-start(bf16[400,128]{1,0:T(8,128)(2,1)S(1)} %collective-permute-done.1.refs_2_), channel_id=1, source_target_pairs={{0,1},{1,0},{2,3},{3,2},{4,5},{5,4},{6,7},{7,6},{8,9},{9,8},{10,11... | collective-permute-start | bytes 307208 | tf_op jit(solution)/shard_map/ppermute | solution.py:237
  20.4 3.8 %collective-permute-start.14 = (bf16[400,128]{1,0:T(8,128)(2,1)S(1)}, bf16[400,128]{1,0:T(8,128)(2,1)S(1)}, u32[]{:S(2)}, u32[]{:S(2)}) collective-permute-start(bf16[400,128]{1,0:T(8,128)(2,1)S(1)} %collective-permute-done.6.refs_7_), channel_id=1, source_target_pairs={{0,1},{1,0},{2,3},{3,2},{4,5},{5,4},{6,7},{7,6},{8,9},{9,8},{10,11... | collective-permute-start | bytes 307208 | tf_op jit(solution)/shard_map/ppermute | solution.py:237
  21.7 2.5 %collective-permute-start.13 = (bf16[400,128]{1,0:T(8,128)(2,1)S(1)}, bf16[400,128]{1,0:T(8,128)(2,1)S(1)}, u32[]{:S(2)}, u32[]{:S(2)}) collective-permute-start(bf16[400,128]{1,0:T(8,128)(2,1)S(1)} %collective-permute-done.5.refs_6_), channel_id=1, source_target_pairs={{0,1},{1,0},{2,3},{3,2},{4,5},{5,4},{6,7},{7,6},{8,9},{9,8},{10,11... | collective-permute-start | bytes 307208 | tf_op jit(solution)/shard_map/ppermute | solution.py:237
  22.6 1.6 %collective-permute-start.12 = (bf16[400,128]{1,0:T(8,128)(2,1)S(1)}, bf16[400,128]{1,0:T(8,128)(2,1)S(1)}, u32[]{:S(2)}, u32[]{:S(2)}) collective-permute-start(bf16[400,128]{1,0:T(8,128)(2,1)S(1)} %collective-permute-done.4.refs_5_), channel_id=1, source_target_pairs={{0,1},{1,0},{2,3},{3,2},{4,5},{5,4},{6,7},{7,6},{8,9},{9,8},{10,11... | collective-permute-start | bytes 307208 | tf_op jit(solution)/shard_map/ppermute | solution.py:237
